TPU v7x, 32 devices: a whole 2x2x4 slice. The times are simulated.
32 devices in a mesh: pair: 4 (over y, x), blk: 4 (over z), rep: 2 (over core).
Axes of the slice: x: 2, y: 2, z: 4, core: 2. Of those that a mesh axis runs over, the one named last changes fastest.
Arguments:
- amplitudes: float32 [12, 80, 608, 608], P(None, ('blk', 'rep'), None, 'pair'), may hold values from -6 to 6
- integrals: float32 [80, 608, 1, 608], P(('blk', 'rep')), may hold values from -0.0390625 to 0.0390625
- virt_sizes: int32 [8], replicated, may hold values from 1 to 152, 608 in all
- i_irrep: int32 [12], replicated, may hold values from 0 to 7
- j_irrep: int32 [1], replicated, may hold values from 0 to 7
Outputs:
- residual: float32 [12, 608, 1, 608], P(None, 'pair', None, ('blk', 'rep'))
Inputs may be any that keep to these rules, and one draw needn't show every extreme that they name: `virt_sizes`: the entries sum to 608.
All inputs are finite; a program needn't handle non-finite values.
Results may differ from a plain program's by a relative error of at most 0.00016.
Values sent between devices are 32-bit elements; how exact they have to be, the bound alone decides.
A program may use at most 320 MiB of HBM per device.

v0:
```python
import functools

import jax
import jax.numpy as jnp
from jax import lax
from jax.experimental import pallas as pl
from jax.experimental.pallas import tpu as pltpu
from jax.sharding import PartitionSpec as P

MESH = pl.DeviceIdType.MESH
VMEM_LIMIT = 60 * 1024 * 1024


def round_up(value, step):
    return -(-value // step) * step


def split_bf16(x):
    high = x.astype(jnp.bfloat16)
    return high, (x - high.astype(jnp.float32)).astype(jnp.bfloat16)


GROUP = 4
STEP = 2


def contract(step, fold, reps, pairs, width, key_ref, row_ref, col_ref, a_ref, w_ref, p_ref, x_hi, x_lo, w_hi, w_lo, acc):
    depth, virt = a_ref.shape[1:]
    stride = x_hi.shape[1] // STEP
    here = virt // pairs

    @pl.when(step == 0)
    def _():
        x_hi[...] = jnp.zeros_like(x_hi)
        x_lo[...] = jnp.zeros_like(x_lo)
        w_hi[...] = jnp.zeros_like(w_hi)
        w_lo[...] = jnp.zeros_like(w_lo)
        p_ref[...] = jnp.zeros_like(p_ref)
        high, low = split_bf16(w_ref[...].T)
        w_hi[:, :depth] = high
        w_lo[:, :depth] = low

    for n in range(STEP):
        high, low = split_bf16(a_ref[n])
        x_hi[:depth, n * stride:n * stride + virt] = high
        x_lo[:depth, n * stride:n * stride + virt] = low
    dot = functools.partial(jnp.dot, preferred_element_type=jnp.float32)
    for start in range(0, x_hi.shape[1], 256):
        high = x_hi[:, start:start + 256]
        acc[:, start:start + 256] = dot(w_hi[...], high) + dot(w_lo[...], high) + dot(w_hi[...], x_lo[:, start:start + 256])

    per_rep = fold // reps
    parts = fold // width // reps
    rounds = GROUP // STEP

    group = lax.div(step, rounds)

    for turn in range(rounds):
        @pl.when(lax.rem(step, rounds) == turn)
        def _(turn=turn):
            for n in range(STEP):
                keep = row_ref[...] == jnp.bitwise_xor(col_ref[...], key_ref[step * STEP + n])
                kept = jnp.where(keep, acc[:, n * stride:n * stride + virt], jnp.float32(0.0))
                slots = kept[:fold]
                for start in range(fold, virt, fold):
                    slots = slots + kept[start:start + fold]
                lane = (turn * STEP + n) * here
                for rep in range(reps):
                    for part in range(parts):
                        source = (part * reps + rep) * width
                        for q in range(pairs):
                            p_ref[rep, q, group, part * width:(part + 1) * width, lane:lane + here] = (
                                slots[source:source + width, q * here:(q + 1) * here])


def cycle_kernel(fold, reps, pairs, blks, width, key_ref, row_ref, col_ref, a_ref, w_ref, o_ref,
                 x_hi, x_lo, w_hi, w_lo, acc, p_ref, own, from_rep, from_pair, right_out, left_out, right_in, left_in,
                 rep_send, rep_recv, pair_send, pair_recv, right_send, right_recv, left_send, left_recv):
    now = pl.program_id(0)
    me = lax.axis_index("pair")
    z = lax.axis_index("blk")
    rep = lax.axis_index("rep")
    bits = [1 << n for n in range(pairs.bit_length() - 1)]
    groups, height = own.shape[1:3]
    chunks = 2 * groups
    size = height // 2
    ahead, behind = lax.rem(z + 1, blks), lax.rem(z + blks - 1, blks)

    def flipped(mask):
        value = 0
        for bit in bits:
            has = lax.rem(lax.div(me, bit), 2)
            value = value + (1 - has if mask & bit else has) * bit
        return value

    block = [flipped(mask) for mask in range(pairs)]
    order = sorted(range(pairs), key=lambda mask: (-bin(mask).count("1"), mask))

    @pl.when(now == 0)
    def _():
        barrier = pltpu.get_barrier_semaphore()
        peers = [{"rep": 1 - rep}, {"blk": ahead}, {"blk": behind}] + [{"pair": block[bit]} for bit in bits]
        for peer in peers:
            pl.semaphore_signal(barrier, inc=1, device_id=peer, device_id_type=MESH)
        pl.semaphore_wait(barrier, len(peers))

        @pl.when(z == 0)
        def _():
            right_in[...] = jnp.zeros_like(right_in)

        @pl.when(z == blks - 1)
        def _():
            left_in[...] = jnp.zeros_like(left_in)

    contract(now, fold, reps, pairs, width, key_ref, row_ref, col_ref, a_ref, w_ref, p_ref, x_hi, x_lo, w_hi, w_lo, acc)

    def span(c):
        return c // 2, pl.ds(c % 2 * size, size)

    def bits_of(c):
        return bits if c % 2 == 0 else bits[::-1]

    def combos(c, phase):
        found = [0]
        for bit in bits_of(c)[phase + 1:]:
            found = found + [mask | bit for mask in found]
        return found

    def slot_of(c, phase, mask):
        return sum(len(combos(c, before)) for before in range(phase)) + combos(c, phase).index(mask)

    def swap(group, mask):
        here = block[mask]
        return pltpu.make_async_remote_copy(
            src_ref=p_ref.at[1 - rep, here, group], dst_ref=from_rep.at[here, group], send_sem=rep_send.at[group, mask],
            recv_sem=rep_recv.at[group, mask], device_id={"rep": 1 - rep}, device_id_type=MESH)

    def halving(c, phase, mask):
        bit = bits_of(c)[phase]
        slot = slot_of(c, phase, mask)
        return pltpu.make_async_remote_copy(
            src_ref=own.at[(block[mask | bit],) + span(c)], dst_ref=from_pair.at[(slot,) + span(c)],
            send_sem=pair_send.at[slot, c], recv_sem=pair_recv.at[slot, c],
            device_id={"pair": block[bit]}, device_id_type=MESH)

    def passing(c, right):
        out, into = (right_out, right_in) if right else (left_out, left_in)
        send, recv = (right_send, right_recv) if right else (left_send, left_recv)
        return pltpu.make_async_remote_copy(
            src_ref=out.at[span(c)], dst_ref=into.at[span(c)], send_sem=send.at[c], recv_sem=recv.at[c],
            device_id={"blk": ahead if right else behind}, device_id_type=MESH)

    def step(c, right):
        out, into = (right_out, right_in) if right else (left_out, left_in)

        @pl.when(z > 0 if right else z < blks - 1)
        def _():
            passing(c, right).wait_recv()

        @pl.when(z < blks - 1 if right else z > 0)
        def _():
            out[span(c)] = own[(block[0],) + span(c)] + into[span(c)]
            passing(c, right).start()

    def start_swaps(group):
        for mask in order:
            swap(group, mask).start()

    def add_swaps(group):
        for mask in order:
            swap(group, mask).wait_recv()
            here = block[mask]
            own[here, group] = p_ref[rep, here, group] + from_rep[here, group]
            for c in (2 * group, 2 * group + 1):
                bit = bits_of(c)[0]
                if mask & bit:
                    halving(c, 0, mask ^ bit).start()

    def add_pairs(group, phases):
        for phase in phases:
            last = phase == len(bits) - 1
            for c in (2 * group, 2 * group + 1):
                following = 0 if last else bits_of(c)[phase + 1]
                for mask in sorted(combos(c, phase), key=lambda mask: -(mask & following)):
                    halving(c, phase, mask).wait_recv()
                    at = (block[mask],) + span(c)
                    own[at] = own[at] + from_pair[(slot_of(c, phase, mask),) + span(c)]
                    if mask & following:
                        halving(c, phase + 1, mask ^ following).start()
                if last:
                    @pl.when(z == 0)
                    def _(c=c):
                        step(c, True)

                    @pl.when(z == blks - 1)
                    def _(c=c):
                        step(c, False)

    def pass_on(first, stop):
        for right in (True, False):
            @pl.when(z < blks // 2 if right else z >= blks // 2)
            def _(right=right):
                for c in range(first, stop + 1):
                    if c < stop:
                        @pl.when(z > 0 if right else z < blks - 1)
                        def _(c=c):
                            step(c, right)
                    if c > first:
                        step(c - 1, not right)

    early, late = range(len(bits) - 1), range(len(bits) - 1, len(bits))
    rounds = GROUP // STEP
    final = groups * rounds - 1

    for group in range(groups):
        ready = (group + 1) * rounds - 1
        following = group + 1 < groups

        @pl.when(now == ready)
        def _(group=group, following=following):
            if group > 0:
                add_pairs(group - 1, early)
            start_swaps(group)
            if not following:
                if group > 0:
                    add_pairs(group - 1, late)
                add_swaps(group)
                pass_on(0, 2 * group)
                add_pairs(group, early)
                add_pairs(group, late)
                pass_on(2 * group, 2 * group + 2)

        if following:
            @pl.when(now == ready + 1)
            def _(group=group):
                if group > 0:
                    add_pairs(group - 1, late)
                add_swaps(group)

    @pl.when(now == final)
    def _():
        here, per_rep = o_ref.shape[1:]
        for i in range(o_ref.shape[0]):
            total = own[block[0], i // GROUP] + right_in[i // GROUP] + left_in[i // GROUP]
            o_ref[i] = total[:, i % GROUP * here:(i % GROUP + 1) * here].T[:, :per_rep]
        for group in range(groups):
            for mask in order:
                swap(group, mask).wait_send()
        for c in range(chunks):
            for phase in range(len(bits)):
                for mask in combos(c, phase):
                    halving(c, phase, mask).wait_send()

            @pl.when(z < blks - 1)
            def _(c=c):
                passing(c, True).wait_send()

            @pl.when(z > 0)
            def _(c=c):
                passing(c, False).wait_send()


def per_device(pairs, blks, reps, amplitudes, integrals, virt_sizes, i_irrep, j_irrep):
    ni, nk, virt, nc = amplitudes.shape
    width = virt // (blks * reps)
    here = virt // pairs
    fold = virt // 4
    per_rep = fold // reps
    height = round_up(per_rep, 8)
    packed = round_up(GROUP * here, 128)
    stride = round_up(virt, 128)
    depth = nk * nc
    deep = round_up(depth, 256)

    ends = jnp.cumsum(virt_sizes)
    irrep = jnp.sum((jnp.arange(virt, dtype=jnp.int32)[:, None] >= ends[None, :]).astype(jnp.int32), axis=1)
    pair = lax.axis_index("pair")
    weights = lax.dynamic_slice_in_dim(integrals, pair * nc, nc, axis=1).reshape(nk * nc, virt)

    groups = ni // GROUP
    chunks = 2 * groups
    dma = pltpu.SemaphoreType.DMA
    block = (groups, height, packed)
    cycle = pl.pallas_call(
        functools.partial(cycle_kernel, fold, reps, pairs, blks, width),
        out_shape=jax.ShapeDtypeStruct((ni, here, per_rep), jnp.float32),
        grid=(ni // STEP,),
        in_specs=[
            pl.BlockSpec(memory_space=pltpu.SMEM),
            pl.BlockSpec((virt, 1), lambda t: (0, 0)),
            pl.BlockSpec((1, virt), lambda t: (0, 0)),
            pl.BlockSpec((STEP, depth, virt), lambda t: (t, 0, 0)),
            pl.BlockSpec((depth, virt), lambda t: (0, 0), pipeline_mode=pl.Buffered(1)),
        ],
        out_specs=pl.BlockSpec((ni, here, per_rep), lambda t: (0, 0, 0), pipeline_mode=pl.Buffered(1)),
        scratch_shapes=[
            pltpu.VMEM((deep, STEP * stride), jnp.bfloat16),
            pltpu.VMEM((deep, STEP * stride), jnp.bfloat16),
            pltpu.VMEM((virt, deep), jnp.bfloat16),
            pltpu.VMEM((virt, deep), jnp.bfloat16),
            pltpu.VMEM((virt, STEP * stride), jnp.float32),
            pltpu.VMEM((reps, pairs) + block, jnp.float32),
            pltpu.VMEM((pairs,) + block, jnp.float32),
            pltpu.VMEM((pairs,) + block, jnp.float32),
            pltpu.VMEM((pairs - 1,) + block, jnp.float32),
        ] + [pltpu.VMEM(block, jnp.float32)] * 4 + [
            dma((groups, pairs)), dma((groups, pairs)),
            dma((pairs - 1, chunks)), dma((pairs - 1, chunks)),
            dma((chunks,)), dma((chunks,)), dma((chunks,)), dma((chunks,)),
        ],
        compiler_params=pltpu.CompilerParams(dimension_semantics=("arbitrary",), collective_id=0,
                                             has_side_effects=True, vmem_limit_bytes=VMEM_LIMIT),
    )(i_irrep, jnp.bitwise_xor(irrep, j_irrep[0])[:, None], irrep[None, :],
      jnp.swapaxes(amplitudes, 2, 3).reshape(ni, depth, virt), weights)

    blk = lax.axis_index("blk")
    if per_rep > width:
        cycle = lax.dynamic_slice_in_dim(cycle, lax.rem(blk, per_rep // width) * width, width, axis=2)
    owner = blk * reps + lax.axis_index("rep")
    row_irrep = lax.dynamic_slice_in_dim(irrep, pair * here, here)
    col_irrep = lax.dynamic_slice_in_dim(irrep, owner * width, width)
    left = jnp.bitwise_xor(i_irrep[:, None], row_irrep[None, :])
    right = jnp.bitwise_xor(j_irrep[:, None], col_irrep[None, :])
    keep = left[:, :, None, None] == right[None, None, :, :]
    return jnp.where(keep, cycle[:, :, None, :], jnp.float32(0.0))


def solution(mesh):
    return jax.shard_map(
        functools.partial(per_device, mesh.shape["pair"], mesh.shape["blk"], mesh.shape["rep"]),
        mesh=mesh,
        in_specs=(
            P(None, ("blk", "rep"), None, "pair"),
            P(("blk", "rep"), None, None, None),
            P(),
            P(),
            P(),
        ),
        out_specs=P(None, "pair", None, ("blk", "rep")),
        check_vma=False,
    )
```

profile of v0, /device:TPU:0, one launch (start us, length us, event | category | flops | bytes accessed | tf_op | source)
XLA Modules:
  0.0 112.0 jit_solution(16926951691580460315)
XLA Ops:
  0.0 0.8 reduce-window.8
  0.8 0.1 convert_reduce_fusion
  1.6 0.1 dynamic-slice_xor_fusion
  1.6 4.8 %constant_dynamic-slice_fusion = f32[10,152,1,608]{3,2,1,0:T(1,128)S(1)} fusion(f32[10,608,1,608]{3,2,1,0:T(1,128)} %param.6, s32[]{:T(128)S(6)} %select_n.14), kind=kLoop, calls=%fused_computation.6 | loop fusion | bytes 7393284 | tf_op jit(solution)/shard_map/dynamic_slice | solution.py:278
  6.4 2.1 %copy.11 = f32[10,152,1,608]{3,1,2,0:T(8,128)} copy(f32[10,152,1,608]{3,2,1,0:T(1,128)S(1)} %constant_dynamic-slice_fusion) | data formatting | bytes 7393280
  8.5 0.9 xor.53.row_ref
  9.4 0.6 broadcast_in_dim.5.col_ref
  10.0 0.0 copy-start
  10.0 99.4 %shard_map.55 = f32[12,152,76]{2,1,0:T(8,128)} custom-call(s32[12]{0:T(128)} %key_ref.1, s32[608,1]{1,0:T(8,128)} %xor.53.row_ref, s32[1,608]{1,0:T(1,128)} %broadcast_in_dim.5.col_ref, f32[12,1520,608]{2,1,0:T(8,128)} %bitcast.12, f32[1520,608]{1,0:T(8,128)} %bitcast.13), custom_call_target="tpu_custom_call" | custom-call | tf_op jit(solution)/shard_map/pallas_call | solution.py:284
  109.4 0.1 dynamic_slice.9
  109.5 0.0 copy-done
  109.5 0.1 broadcast_xor_fusion
  109.6 2.4 %compare_select_fusion = f32[12,152,76]{2,1,0:T(8,128)} fusion(f32[12,152,76]{2,1,0:T(8,128)} %shard_map.55, s32[76]{0:T(128)S(1)} %dynamic-slice_xor_fusion, s32[12,152]{1,0:T(8,128)S(1)} %broadcast_xor_fusion), kind=kLoop, calls=%fused_computation | loop fusion | flops 277248 | bytes 1116592 | tf_op jit(solution)/shard_map/jit(_where)/select_n | solution.py:325
  (1 shorter events, 0.0 us)
Async XLA Ops:
  10.0 99.5 %copy-start = (s32[12]{0:T(128)S(1)}, s32[12]{0:T(128)}, u32[]{:S(2)}) copy-start(s32[12]{0:T(128)} %key_ref.1) | copy-start | bytes 148
where the time goes:
time: 112 us
  Pallas kernels  99.4 us (89%)
  local copies, waits for them, and re-layouts  8.43 us (8%)
  other arithmetic  3.49 us (3%)
    pallas_call x1, Pallas kernels, per_device(): pl.pallas_call(functools.partial(cycle_kernel, fold, reps, pairs, blks, w...  99.4 us
    dynamic_slice x1, local copies, waits for them, and re-layouts, per_device(): lax.dynamic_slice_in_dim(integrals, pair * nc, nc, axis=1)  4.77 us
    select_n x1, other arithmetic, per_device(): return jnp.where(keep, cycle[:, :, None, :], jnp.float32(0.0))  2.42 us

commit v1 on v0

--- a/solution.py
+++ b/solution.py
@@ -22,34 +22,79 @@
 
 GROUP = 4
 STEP = 2
-
-
-def contract(step, fold, reps, pairs, width, key_ref, row_ref, col_ref, a_ref, w_ref, p_ref, x_hi, x_lo, w_hi, w_lo, acc):
+F8 = jnp.float8_e4m3fn
+TOP = 256.0
+LEAST = 1e-30
+
+
+def largest(x):
+    rows = x.shape[0]
+    most = jnp.abs(x[:16])
+    for start in [*range(16, rows - 15, 16)] + ([rows - 16] if rows % 16 else []):
+        most = jnp.maximum(most, jnp.abs(x[start:start + 16]))
+    return jnp.maximum(jnp.max(most.astype(jnp.float32)), jnp.float32(LEAST))
+
+
+def splat(value, shape):
+    return jnp.full(shape, value, jnp.float32).astype(jnp.bfloat16)
+
+
+def rounded(value):
+    return jnp.max(splat(value, (16, 128)).astype(jnp.float32))
+
+
+def irrep_of(index, sizes_ref):
+    end, value = jnp.int32(0), jnp.zeros_like(index)
+    for n in range(sizes_ref.shape[0]):
+        end = end + sizes_ref[n]
+        value = value + (index >= end).astype(jnp.int32)
+    return value
+
+
+def load_weights(w_ref, w_hi, w_lo, w_8, w_scale):
+    nk, nc, virt = w_ref.shape
+    depth, deep = nk * nc, w_hi.shape[1]
+    high, low = split_bf16(jnp.concatenate([w_ref[k] for k in range(nk)], axis=0).T)
+    w_hi[:, depth:] = jnp.zeros((virt, deep - depth), jnp.bfloat16)
+    w_lo[:, depth:] = jnp.zeros((virt, deep - depth), jnp.bfloat16)
+    w_hi[:, :depth] = high
+    w_lo[:, :depth] = low
+    scale = rounded(TOP / largest(high))
+    w_scale[0] = scale
+    w_8[:, :deep] = (w_hi[...] * splat(scale, w_hi.shape)).astype(F8)
+    w_8[:, deep:] = (w_lo[...] * splat(scale * TOP, w_lo.shape)).astype(F8)
+
+
+def contract(step, fold, reps, pairs, width, key_ref, row_s, col_s, a_ref, p_ref, x_hi, x_lo, x_8, w_hi, w_8, w_scale, acc, slots):
     depth, virt = a_ref.shape[1:]
-    stride = x_hi.shape[1] // STEP
+    deep, lanes = x_hi.shape
+    stride = lanes // STEP
     here = virt // pairs
 
-    @pl.when(step == 0)
-    def _():
-        x_hi[...] = jnp.zeros_like(x_hi)
-        x_lo[...] = jnp.zeros_like(x_lo)
-        w_hi[...] = jnp.zeros_like(w_hi)
-        w_lo[...] = jnp.zeros_like(w_lo)
-        p_ref[...] = jnp.zeros_like(p_ref)
-        high, low = split_bf16(w_ref[...].T)
-        w_hi[:, :depth] = high
-        w_lo[:, :depth] = low
-
+    most = []
     for n in range(STEP):
         high, low = split_bf16(a_ref[n])
+        most.append(largest(high))
         x_hi[:depth, n * stride:n * stride + virt] = high
         x_lo[:depth, n * stride:n * stride + virt] = low
     dot = functools.partial(jnp.dot, preferred_element_type=jnp.float32)
-    for start in range(0, x_hi.shape[1], 256):
-        high = x_hi[:, start:start + 256]
-        acc[:, start:start + 256] = dot(w_hi[...], high) + dot(w_lo[...], high) + dot(w_hi[...], x_lo[:, start:start + 256])
-
-    per_rep = fold // reps
+    for start in range(0, lanes, 256):
+        acc[:, start:start + 256] = dot(w_hi[...], x_hi[:, start:start + 256])
+    scale = rounded(TOP / functools.reduce(jnp.maximum, most))
+    x_8[:deep] = (x_lo[...] * splat(scale * TOP, x_lo.shape)).astype(F8)
+    x_8[deep:] = (x_hi[...] * splat(scale, x_hi.shape)).astype(F8)
+    back = (1.0 / scale) * (1.0 / w_scale[0]) * (1.0 / TOP)
+    for start in range(0, lanes, 256):
+        total = acc[:, start:start + 256] + dot(w_8[...], x_8[:, start:start + 256]) * back
+        for lane in (start, start + 128):
+            key = key_ref[step * STEP + lane // stride]
+            keep = row_s[...] == jnp.bitwise_xor(col_s[:, lane % stride:lane % stride + 128], key)
+            kept = jnp.where(keep, total[:, lane - start:lane - start + 128], jnp.float32(0.0))
+            folded = kept[:fold]
+            for first in range(fold, virt, fold):
+                folded = folded + kept[first:first + fold]
+            slots[:, lane:lane + 128] = folded
+
     parts = fold // width // reps
     rounds = GROUP // STEP
 
@@ -59,22 +104,18 @@
         @pl.when(lax.rem(step, rounds) == turn)
         def _(turn=turn):
             for n in range(STEP):
-                keep = row_ref[...] == jnp.bitwise_xor(col_ref[...], key_ref[step * STEP + n])
-                kept = jnp.where(keep, acc[:, n * stride:n * stride + virt], jnp.float32(0.0))
-                slots = kept[:fold]
-                for start in range(fold, virt, fold):
-                    slots = slots + kept[start:start + fold]
+                folded = slots[:, n * stride:n * stride + virt]
                 lane = (turn * STEP + n) * here
                 for rep in range(reps):
                     for part in range(parts):
                         source = (part * reps + rep) * width
                         for q in range(pairs):
                             p_ref[rep, q, group, part * width:(part + 1) * width, lane:lane + here] = (
-                                slots[source:source + width, q * here:(q + 1) * here])
-
-
-def cycle_kernel(fold, reps, pairs, blks, width, key_ref, row_ref, col_ref, a_ref, w_ref, o_ref,
-                 x_hi, x_lo, w_hi, w_lo, acc, p_ref, own, from_rep, from_pair, right_out, left_out, right_in, left_in,
+                                folded[source:source + width, q * here:(q + 1) * here])
+
+
+def cycle_kernel(fold, reps, pairs, blks, width, key_ref, last_ref, sizes_ref, a_any, w_any, o_ref,
+                 row_s, col_s, a_buf, w_buf, a_sem, w_sem, x_hi, x_lo, x_8, w_hi, w_lo, w_8, w_scale, acc, slots, p_ref, own, from_rep, from_pair, right_out, left_out, right_in, left_in,
                  rep_send, rep_recv, pair_send, pair_recv, right_send, right_recv, left_send, left_recv):
     now = pl.program_id(0)
     me = lax.axis_index("pair")
@@ -96,6 +137,27 @@
     block = [flipped(mask) for mask in range(pairs)]
     order = sorted(range(pairs), key=lambda mask: (-bin(mask).count("1"), mask))
 
+    steps = a_any.shape[0] // STEP
+    nk, nc, virt = w_buf.shape
+
+    def fetch(t):
+        slot = lax.rem(t, 2)
+        return pltpu.make_async_copy(a_any.at[pl.ds(t * STEP, STEP)], a_buf.at[slot], a_sem.at[slot])
+
+    def weights(k):
+        return pltpu.make_async_copy(
+            w_any.at[k, pl.ds(me * nc, nc), 0], w_buf.at[k], w_sem.at[k])
+
+    @pl.when(now == 0)
+    def _():
+        for k in range(nk):
+            weights(k).start()
+        fetch(now).start()
+
+    @pl.when(now + 1 < steps)
+    def _():
+        fetch(now + 1).start()
+
     @pl.when(now == 0)
     def _():
         barrier = pltpu.get_barrier_semaphore()
@@ -104,6 +166,26 @@
             pl.semaphore_signal(barrier, inc=1, device_id=peer, device_id_type=MESH)
         pl.semaphore_wait(barrier, len(peers))
 
+        depth, lanes = a_buf.shape[2], x_hi.shape[1]
+        stride = lanes // STEP
+        for ref in (x_hi, x_lo):
+            ref[depth:] = jnp.zeros((ref.shape[0] - depth, lanes), jnp.bfloat16)
+            for n in range(STEP):
+                ref[:, n * stride + virt:(n + 1) * stride] = jnp.zeros((ref.shape[0], stride - virt), jnp.bfloat16)
+        tall, wide = p_ref.shape[3:]
+        used = virt // pairs * GROUP
+        here_rows = fold // reps
+        if here_rows < tall:
+            p_ref[:, :, :, here_rows:] = jnp.zeros(p_ref.shape[:3] + (tall - here_rows, wide), jnp.float32)
+        if used < wide:
+            p_ref[:, :, :, :, used:] = jnp.zeros(p_ref.shape[:4] + (wide - used,), jnp.float32)
+        row_s[...] = jnp.bitwise_xor(
+            irrep_of(lax.broadcasted_iota(jnp.int32, row_s.shape, 0), sizes_ref), last_ref[0])
+        col_s[...] = irrep_of(lax.broadcasted_iota(jnp.int32, col_s.shape, 1), sizes_ref)
+        for k in range(nk):
+            weights(k).wait()
+        load_weights(w_buf, w_hi, w_lo, w_8, w_scale)
+
         @pl.when(z == 0)
         def _():
             right_in[...] = jnp.zeros_like(right_in)
@@ -112,7 +194,9 @@
         def _():
             left_in[...] = jnp.zeros_like(left_in)
 
-    contract(now, fold, reps, pairs, width, key_ref, row_ref, col_ref, a_ref, w_ref, p_ref, x_hi, x_lo, w_hi, w_lo, acc)
+    fetch(now).wait()
+    contract(now, fold, reps, pairs, width, key_ref, row_s, col_s, a_buf.at[lax.rem(now, 2)], p_ref,
+             x_hi, x_lo, x_8, w_hi, w_8, w_scale, acc, slots)
 
     def span(c):
         return c // 2, pl.ds(c % 2 * size, size)
@@ -240,9 +324,14 @@
     @pl.when(now == final)
     def _():
         here, per_rep = o_ref.shape[1:]
+        shift = (z * reps + rep) * width - lax.rem(z, per_rep // width) * width
+        left = irrep_of(me * here + lax.broadcasted_iota(jnp.int32, (here, per_rep), 0), sizes_ref)
+        right = jnp.bitwise_xor(
+            irrep_of(shift + lax.broadcasted_iota(jnp.int32, (here, per_rep), 1), sizes_ref), last_ref[0])
         for i in range(o_ref.shape[0]):
             total = own[block[0], i // GROUP] + right_in[i // GROUP] + left_in[i // GROUP]
-            o_ref[i] = total[:, i % GROUP * here:(i % GROUP + 1) * here].T[:, :per_rep]
+            value = total[:, i % GROUP * here:(i % GROUP + 1) * here].T[:, :per_rep]
+            o_ref[i] = jnp.where(jnp.bitwise_xor(left, key_ref[i]) == right, value, jnp.float32(0.0))
         for group in range(groups):
             for mask in order:
                 swap(group, mask).wait_send()
@@ -272,11 +361,6 @@
     depth = nk * nc
     deep = round_up(depth, 256)
 
-    ends = jnp.cumsum(virt_sizes)
-    irrep = jnp.sum((jnp.arange(virt, dtype=jnp.int32)[:, None] >= ends[None, :]).astype(jnp.int32), axis=1)
-    pair = lax.axis_index("pair")
-    weights = lax.dynamic_slice_in_dim(integrals, pair * nc, nc, axis=1).reshape(nk * nc, virt)
-
     groups = ni // GROUP
     chunks = 2 * groups
     dma = pltpu.SemaphoreType.DMA
@@ -285,20 +369,23 @@
         functools.partial(cycle_kernel, fold, reps, pairs, blks, width),
         out_shape=jax.ShapeDtypeStruct((ni, here, per_rep), jnp.float32),
         grid=(ni // STEP,),
-        in_specs=[
-            pl.BlockSpec(memory_space=pltpu.SMEM),
-            pl.BlockSpec((virt, 1), lambda t: (0, 0)),
-            pl.BlockSpec((1, virt), lambda t: (0, 0)),
-            pl.BlockSpec((STEP, depth, virt), lambda t: (t, 0, 0)),
-            pl.BlockSpec((depth, virt), lambda t: (0, 0), pipeline_mode=pl.Buffered(1)),
-        ],
+        in_specs=[pl.BlockSpec(memory_space=pltpu.SMEM)] * 3 + [pl.BlockSpec(memory_space=pl.ANY)] * 2,
         out_specs=pl.BlockSpec((ni, here, per_rep), lambda t: (0, 0, 0), pipeline_mode=pl.Buffered(1)),
         scratch_shapes=[
+            pltpu.VMEM((virt, 128), jnp.int32),
+            pltpu.VMEM((1, stride), jnp.int32),
+            pltpu.VMEM((2, STEP, depth, virt), jnp.float32),
+            pltpu.VMEM((nk, nc, virt), jnp.float32),
+            dma((2,)), dma((nk,)),
             pltpu.VMEM((deep, STEP * stride), jnp.bfloat16),
             pltpu.VMEM((deep, STEP * stride), jnp.bfloat16),
+            pltpu.VMEM((2 * deep, STEP * stride), F8),
             pltpu.VMEM((virt, deep), jnp.bfloat16),
             pltpu.VMEM((virt, deep), jnp.bfloat16),
+            pltpu.VMEM((virt, 2 * deep), F8),
+            pltpu.SMEM((1,), jnp.float32),
             pltpu.VMEM((virt, STEP * stride), jnp.float32),
+            pltpu.VMEM((fold, STEP * stride), jnp.float32),
             pltpu.VMEM((reps, pairs) + block, jnp.float32),
             pltpu.VMEM((pairs,) + block, jnp.float32),
             pltpu.VMEM((pairs,) + block, jnp.float32),
@@ -310,19 +397,12 @@
         ],
         compiler_params=pltpu.CompilerParams(dimension_semantics=("arbitrary",), collective_id=0,
                                              has_side_effects=True, vmem_limit_bytes=VMEM_LIMIT),
-    )(i_irrep, jnp.bitwise_xor(irrep, j_irrep[0])[:, None], irrep[None, :],
-      jnp.swapaxes(amplitudes, 2, 3).reshape(ni, depth, virt), weights)
-
-    blk = lax.axis_index("blk")
+    )(i_irrep, j_irrep, virt_sizes, jnp.swapaxes(amplitudes, 2, 3).reshape(ni, depth, virt), integrals)
+
     if per_rep > width:
-        cycle = lax.dynamic_slice_in_dim(cycle, lax.rem(blk, per_rep // width) * width, width, axis=2)
-    owner = blk * reps + lax.axis_index("rep")
-    row_irrep = lax.dynamic_slice_in_dim(irrep, pair * here, here)
-    col_irrep = lax.dynamic_slice_in_dim(irrep, owner * width, width)
-    left = jnp.bitwise_xor(i_irrep[:, None], row_irrep[None, :])
-    right = jnp.bitwise_xor(j_irrep[:, None], col_irrep[None, :])
-    keep = left[:, :, None, None] == right[None, None, :, :]
-    return jnp.where(keep, cycle[:, :, None, :], jnp.float32(0.0))
+        part = lax.rem(lax.axis_index("blk"), per_rep // width)
+        cycle = lax.dynamic_slice_in_dim(cycle, part * width, width, axis=2)
+    return cycle[:, :, None, :]
 
 
 def solution(mesh):

time: 112 us -> 87.2 us (0.78)
  Pallas kernels: 99.4 us -> 84.2 us
  local copies, waits for them, and re-layouts: 8.43 us -> 2.17 us
  other arithmetic: 3.49 us -> 0 us
    pallas_call x1, Pallas kernels: 99.4 us -> 84.2 us  [per_device(): pl.pallas_call(functools.partial(cycle_kernel, fold, reps, pairs, blks, w...]
    dynamic_slice x2 -> x0, local copies, waits for them, and re-layouts: 4.85 us -> none  [the longest x1 4.77 us: per_device(): lax.dynamic_slice_in_dim(integrals, pair * nc, nc, axis=1)]
    select_n x1 -> x0, other arithmetic: 2.42 us -> none  [per_device(): return jnp.where(keep, cycle[:, :, None, :], jnp.float32(0.0))]
where the time goes in v1:
time: 87.2 us; the launch traced here: 87.1 us
  Pallas kernels  84.2 us (97%)
  local copies, waits for them, and re-layouts  2.17 us (2%)
    pallas_call x1, Pallas kernels, per_device(): pl.pallas_call(functools.partial(cycle_kernel, fold, reps, pairs, blks, w...  84.2 us
    unnamed x1, local copies, waits for them, and re-layouts  2.17 us

profile of v1, /device:TPU:0, one launch (start us, length us, event | category | flops | bytes accessed | tf_op | source)
XLA Modules:
  0.0 87.1 jit_solution(816226563597649456)
XLA Ops:
  0.7 84.2 %shard_map.55 = f32[12,152,76]{2,1,0:T(8,128)} custom-call(s32[12]{0:T(128)} %key_ref.1, s32[1]{0:T(128)S(6)} %copy.8.last_ref, s32[8]{0:T(128)} %sizes_ref.1, f32[12,1520,608]{2,1,0:T(8,128)} %bitcast.6, f32[10,608,1,608]{3,2,1,0:T(1,128)} %w_any.1), custom_call_target="tpu_custom_call" | custom-call | tf_op jit(solution)/shard_map/pallas_call | solution.py:368
  84.9 2.2 %copy.9 = f32[12,152,1,76]{3,2,1,0:T(1,128)} copy(f32[12,152,1,76]{3,2,1,0:T(1,128)} %bitcast.7) | data formatting | bytes 1108992

commit v2 on v1

--- a/solution.py
+++ b/solution.py
@@ -20,8 +20,8 @@
     return high, (x - high.astype(jnp.float32)).astype(jnp.bfloat16)
 
 
-GROUP = 4
-STEP = 2
+GROUP = 2
+STEP = GROUP
 F8 = jnp.float8_e4m3fn
 TOP = 256.0
 LEAST = 1e-30
@@ -96,22 +96,14 @@
             slots[:, lane:lane + 128] = folded
 
     parts = fold // width // reps
-    rounds = GROUP // STEP
-
-    group = lax.div(step, rounds)
-
-    for turn in range(rounds):
-        @pl.when(lax.rem(step, rounds) == turn)
-        def _(turn=turn):
-            for n in range(STEP):
-                folded = slots[:, n * stride:n * stride + virt]
-                lane = (turn * STEP + n) * here
-                for rep in range(reps):
-                    for part in range(parts):
-                        source = (part * reps + rep) * width
-                        for q in range(pairs):
-                            p_ref[rep, q, group, part * width:(part + 1) * width, lane:lane + here] = (
-                                folded[source:source + width, q * here:(q + 1) * here])
+    for n in range(STEP):
+        folded = slots[:, n * stride:n * stride + virt]
+        for rep in range(reps):
+            for part in range(parts):
+                source = (part * reps + rep) * width
+                for q in range(pairs):
+                    p_ref[rep, q, step, part * width:(part + 1) * width, n * here:(n + 1) * here] = (
+                        folded[source:source + width, q * here:(q + 1) * here])
 
 
 def cycle_kernel(fold, reps, pairs, blks, width, key_ref, last_ref, sizes_ref, a_any, w_any, o_ref,
@@ -260,66 +252,48 @@
                 if mask & bit:
                     halving(c, 0, mask ^ bit).start()
 
-    def add_pairs(group, phases):
-        for phase in phases:
-            last = phase == len(bits) - 1
-            for c in (2 * group, 2 * group + 1):
-                following = 0 if last else bits_of(c)[phase + 1]
-                for mask in sorted(combos(c, phase), key=lambda mask: -(mask & following)):
-                    halving(c, phase, mask).wait_recv()
-                    at = (block[mask],) + span(c)
-                    own[at] = own[at] + from_pair[(slot_of(c, phase, mask),) + span(c)]
-                    if mask & following:
-                        halving(c, phase + 1, mask ^ following).start()
-                if last:
-                    @pl.when(z == 0)
-                    def _(c=c):
-                        step(c, True)
-
-                    @pl.when(z == blks - 1)
-                    def _(c=c):
-                        step(c, False)
-
-    def pass_on(first, stop):
+    def add_pairs(group, phase):
+        last = phase == len(bits) - 1
+        for c in (2 * group, 2 * group + 1):
+            following = 0 if last else bits_of(c)[phase + 1]
+            for mask in sorted(combos(c, phase), key=lambda mask: -(mask & following)):
+                halving(c, phase, mask).wait_recv()
+                at = (block[mask],) + span(c)
+                own[at] = own[at] + from_pair[(slot_of(c, phase, mask),) + span(c)]
+                if mask & following:
+                    halving(c, phase + 1, mask ^ following).start()
+            if last:
+                hop(c, 0)
+
+    def hop(c, k):
         for right in (True, False):
-            @pl.when(z < blks // 2 if right else z >= blks // 2)
+            @pl.when(z == (k if right else blks - 1 - k))
             def _(right=right):
-                for c in range(first, stop + 1):
-                    if c < stop:
-                        @pl.when(z > 0 if right else z < blks - 1)
-                        def _(c=c):
-                            step(c, right)
-                    if c > first:
-                        step(c - 1, not right)
-
-    early, late = range(len(bits) - 1), range(len(bits) - 1, len(bits))
-    rounds = GROUP // STEP
-    final = groups * rounds - 1
-
-    for group in range(groups):
-        ready = (group + 1) * rounds - 1
-        following = group + 1 < groups
-
-        @pl.when(now == ready)
-        def _(group=group, following=following):
-            if group > 0:
-                add_pairs(group - 1, early)
-            start_swaps(group)
-            if not following:
-                if group > 0:
-                    add_pairs(group - 1, late)
+                step(c, right)
+
+    def advance(time):
+        for group in range(groups):
+            age = time - group
+            if age == 0:
+                start_swaps(group)
+            elif age == 1:
                 add_swaps(group)
-                pass_on(0, 2 * group)
-                add_pairs(group, early)
-                add_pairs(group, late)
-                pass_on(2 * group, 2 * group + 2)
-
-        if following:
-            @pl.when(now == ready + 1)
-            def _(group=group):
-                if group > 0:
-                    add_pairs(group - 1, late)
-                add_swaps(group)
+            elif 2 <= age < 2 + len(bits):
+                add_pairs(group, age - 2)
+            elif 2 + len(bits) <= age <= len(bits) + blks:
+                for c in (2 * group, 2 * group + 1):
+                    hop(c, age - 1 - len(bits))
+
+    final = groups - 1
+    for time in range(groups):
+        @pl.when(now == time)
+        def _(time=time):
+            advance(time)
+
+    @pl.when(now == final)
+    def _():
+        for time in range(groups, groups + len(bits) + blks):
+            advance(time)
 
     @pl.when(now == final)
     def _():

time: 87.2 us -> 77.2 us (0.89)
  Pallas kernels: 84.2 us -> 74.2 us
    pallas_call x1, Pallas kernels: 84.2 us -> 74.2 us  [per_device(): pl.pallas_call(functools.partial(cycle_kernel, fold, reps, pairs, blks, w...]
where the time goes in v2:
time: 77.2 us; the launch traced here: 77.1 us
  Pallas kernels  74.2 us (96%)
  local copies, waits for them, and re-layouts  2.17 us (3%)
    pallas_call x1, Pallas kernels, per_device(): pl.pallas_call(functools.partial(cycle_kernel, fold, reps, pairs, blks, w...  74.2 us
    unnamed x1, local copies, waits for them, and re-layouts  2.17 us

profile of v2, /device:TPU:0, one launch (start us, length us, event | category | flops | bytes accessed | tf_op | source)
XLA Modules:
  0.0 77.1 jit_solution(13845690411659876654)
XLA Ops:
  0.7 74.2 %shard_map.55 = f32[12,152,76]{2,1,0:T(8,128)} custom-call(s32[12]{0:T(128)} %key_ref.1, s32[1]{0:T(128)S(6)} %copy.8.last_ref, s32[8]{0:T(128)} %sizes_ref.1, f32[12,1520,608]{2,1,0:T(8,128)} %bitcast.6, f32[10,608,1,608]{3,2,1,0:T(1,128)} %w_any.1), custom_call_target="tpu_custom_call" | custom-call | tf_op jit(solution)/shard_map/pallas_call | solution.py:342
  74.9 2.2 %copy.9 = f32[12,152,1,76]{3,2,1,0:T(1,128)} copy(f32[12,152,1,76]{3,2,1,0:T(1,128)} %bitcast.7) | data formatting | bytes 1108992
